TPU v7x, 512 devices: a whole 4x8x8 slice. The times are simulated.
512 devices in a mesh: seq: 64 (over z, x, y_hi), ch: 8 (over y_lo, core).
Axes of the slice: x: 4, y: 8 (y_hi: 2, y_lo: 4; y = y_hi * 4 + y_lo), z: 8, core: 2. Of those that a mesh axis runs over, the one named last changes fastest.
Arguments:
- queries: bfloat16 [4096, 8192], P('ch', 'seq'), may hold values from -6 to 6
- key_feat: bfloat16 [4096, 8192], P('ch', 'seq'), may hold values from -6 to 6
- value_feat: bfloat16 [4096, 8192], P('ch', 'seq'), may hold values from -6 to 6
- out_grad: bfloat16 [4096, 8192], P('ch', 'seq'), may hold values from -6 to 6
- out_weight: bfloat16 [4096, 4096], P('ch', 'seq'), may hold values from -0.09375 to 0.09375
- long_filter: bfloat16 [4096, 8192], P('ch', 'seq'), may hold values from -0.125 to 0.125
- short_filter: bfloat16 [256, 128], P('ch'), may hold values from -0.5 to 0.5
Outputs:
- d_key: bfloat16 [4096, 8192], P('ch', 'seq')
- d_value: bfloat16 [4096, 8192], P('ch', 'seq')
- d_filter: float32 [256, 128], P('ch')
All inputs are finite; a program needn't handle non-finite values.
Results may differ from a plain program's by a relative error of at most 0.0064.
Values may be sent and summed in bfloat16 or wider, within the bound.
No kernel may reach another device: no remote copies, remote signals or barrier semaphores. Data moves between devices by JAX's collectives and lax.ppermute only.
A program may use at most 64 MiB of HBM per device.

v0:
```python
import math
import jax
import jax.numpy as jnp
from jax import lax
from jax.sharding import PartitionSpec as P

highest = lax.Precision.HIGHEST


def from_behind(value, axis, steps):
    count = lax.axis_size(axis)
    first, last = (max(0, -steps), min(count, count - steps))
    return lax.ppermute(value, axis, [(source, source + steps) for source in range(first, last)])


def angle_table(first, second, modulus):
    left = lax.broadcasted_iota(jnp.int32, (first, second), 0)
    right = lax.broadcasted_iota(jnp.int32, (first, second), 1)
    phase = (left * right % modulus).astype(jnp.float32) * (2.0 * math.pi / modulus)
    return (jnp.cos(phase), jnp.sin(phase))


def contract(form, first, second):
    return jnp.einsum(form, first, second, precision=highest)


def spectral(pair):
    grads, filters = pair
    items = grads.shape[1]
    seq_len = grads.shape[2]
    inner = 128
    half = seq_len // inner
    outer = 2 * half
    total_len = outer * inner
    cos_p, sin_p = angle_table(outer, half, outer)
    cos_t, sin_t = angle_table(outer, inner, total_len)
    cos_q, sin_q = angle_table(inner, inner, inner)

    def forward(signal):
        series = signal.astype(jnp.float32).reshape(items, half, inner)
        first_re = contract("kn,cnq->ckq", cos_p, series)
        first_im = -contract("kn,cnq->ckq", sin_p, series)
        turned_re = first_re * cos_t + first_im * sin_t
        turned_im = first_im * cos_t - first_re * sin_t
        spec_re = contract("ckq,qm->ckm", turned_re, cos_q) + contract(
            "ckq,qm->ckm", turned_im, sin_q
        )
        spec_im = contract("ckq,qm->ckm", turned_im, cos_q) - contract(
            "ckq,qm->ckm", turned_re, sin_q
        )
        return (spec_re, spec_im)

    grad_re, grad_im = forward(grads[0])
    filt_re, filt_im = forward(filters[0])
    prod_re = filt_re * grad_re + filt_im * grad_im
    prod_im = filt_re * grad_im - filt_im * grad_re
    back_re = contract("ckq,qm->ckm", prod_re, cos_q) - contract("ckq,qm->ckm", prod_im, sin_q)
    back_im = contract("ckq,qm->ckm", prod_im, cos_q) + contract("ckq,qm->ckm", prod_re, sin_q)
    twist_re = back_re * cos_t - back_im * sin_t
    twist_im = back_im * cos_t + back_re * sin_t
    result = contract("kn,ckq->cnq", cos_p, twist_re) - contract("kn,ckq->cnq", sin_p, twist_im)
    return (result / total_len).reshape(1, items, seq_len).astype(jnp.bfloat16)


def windows(extended, group_count, per_group, block_count, tap_count):
    parts = extended.reshape(group_count, per_group, block_count + 1, tap_count)
    return jnp.concatenate([parts[:, :, :-1], parts[:, :, 1:]], axis=3)


def local(queries, key_feat, value_feat, out_grad, out_weight, long_filter, short_filter):
    seq_devices = lax.axis_size("seq")
    channels, row_count = out_grad.shape
    group_count, tap_count = short_filter.shape
    per_group = channels // group_count
    block_count = row_count // tap_count
    per_device = channels // seq_devices
    whole = lax.all_gather(out_grad, "ch", axis=0, tiled=True)
    d_z = jnp.dot(
        lax.all_gather(out_weight, "seq", axis=1, tiled=True),
        whole,
        preferred_element_type=jnp.float32,
    )
    d_c = (d_z * queries.astype(jnp.float32)).astype(jnp.bfloat16)
    packed = (
        d_c.reshape(seq_devices, per_device, row_count),
        long_filter.reshape(seq_devices, per_device, row_count),
    )
    d_w = spectral(
        (
            lax.all_to_all(packed[0], "seq", split_axis=0, concat_axis=2, tiled=True),
            lax.all_to_all(packed[1], "seq", split_axis=0, concat_axis=2, tiled=True),
        )
    )
    prev_rows = from_behind(value_feat, "seq", 1)
    ext_values = jnp.concatenate([prev_rows, value_feat], axis=1)
    value_win = windows(ext_values, group_count, per_group, block_count, tap_count)
    padded_filter = jnp.pad(short_filter, ((0, 0), (0, tap_count + 1)))
    toeplitz = jnp.tile(padded_filter, (1, tap_count))[:, : 2 * tap_count * tap_count]
    toeplitz = toeplitz.reshape(group_count, tap_count, 2 * tap_count)
    reversed_out = jnp.einsum(
        "gtw,gcbw->gcbt", toeplitz, value_win[..., ::-1], preferred_element_type=jnp.float32
    )
    filtered = reversed_out[..., ::-1].reshape(channels, row_count)
    back = lax.all_to_all(d_w, "seq", split_axis=2, concat_axis=0, tiled=True)
    d_w_local = back.reshape(channels, row_count)
    d_vf = (d_w_local.astype(jnp.float32) * key_feat.astype(jnp.float32)).astype(jnp.bfloat16)
    ahead = from_behind(d_vf, "seq", -1)
    ext_grads = jnp.concatenate([d_vf, ahead], axis=1)
    d_key = (d_w_local.astype(jnp.float32) * filtered).astype(jnp.bfloat16)
    grad_win = windows(ext_grads, group_count, per_group, block_count, tap_count)
    d_value = jnp.einsum("gtw,gcbw->gcbt", toeplitz, grad_win, preferred_element_type=jnp.float32)
    d_value = d_value.reshape(channels, row_count).astype(jnp.bfloat16)
    grads_blocked = d_vf.reshape(group_count, per_group, block_count, tap_count)
    corr = jnp.einsum(
        "gcbt,gcbw->gtw", grads_blocked, value_win, preferred_element_type=jnp.float32
    )
    flat = corr.reshape(group_count, 2 * tap_count * tap_count)
    flat = jnp.pad(flat, ((0, 0), (0, tap_count)))
    skewed = flat.reshape(group_count, tap_count, 2 * tap_count + 1)
    column_sums = jnp.sum(skewed, axis=1)
    local_part = column_sums[:, 1 : tap_count + 1][:, ::-1]
    summed = lax.psum(local_part, "seq")
    scale_factor = 1.0 / math.sqrt(row_count * seq_devices * per_group)
    return (d_key, d_value, summed * scale_factor)


def solution(mesh):
    placed = (
        P("ch", "seq"),
        P("ch", "seq"),
        P("ch", "seq"),
        P("ch", "seq"),
        P("ch", "seq"),
        P("ch", "seq"),
        P("ch", None),
    )
    return jax.shard_map(
        local,
        mesh=mesh,
        in_specs=placed,
        out_specs=(P("ch", "seq"), P("ch", "seq"), P("ch", None)),
        check_vma=False,
    )
```

profile of v0, /device:TPU:16, one launch (start us, length us, event | category | flops | bytes accessed | tf_op | source)
XLA Modules:
  0.0 815.4 jit_solution(5035333514818780619)
XLA Ops:
  8.6 5.9 collective-permute-start
  14.6 15.8 %all-to-all-start = ((bf16[64,8,128]{2,1,0:T(8,128)(2,1)}), bf16[64,8,128]{2,1,0:T(8,128)(2,1)S(1)}, u32[]{:S(2)}, u32[]{:S(2)}) async-start(bf16[64,8,128]{2,1,0:T(8,128)(2,1)} %bitcast.129), calls=%async_computation | async-start | bytes 262144 | tf_op jit(solution)/shard_map/all_to_all | solution.py:91
  31.6 2.0 tile.4
  33.5 6.2 tile.10
  43.4 3.3 all-to-all-done
  48.6 1.6 convolution_add_fusion.2
  50.2 161.0 %all-gather.3.cloned.1.call-done = bf16[512,4096]{0,1:T(8,128)(2,1)} async-done(((bf16[512,64]{0,1:T(8,128)(2,1)}), bf16[512,4096]{0,1:T(8,128)(2,1)}) %all-gather.3.cloned.1.call-update) | async-done | bytes 4194320 | tf_op jit(solution)/shard_map/all_gather | solution.py:79
  211.2 4.5 fusion.5
  215.7 9.9 %all-to-all-start.1 = ((bf16[64,8,128]{2,1,0:T(8,128)(2,1)}), bf16[64,8,128]{2,1,0:T(8,128)(2,1)S(1)}, u32[]{:S(2)}, u32[]{:S(2)}) async-start(bf16[64,8,128]{2,1,0:T(8,128)(2,1)} %fusion.5), calls=%async_computation.1 | async-start | bytes 262144 | tf_op jit(solution)/shard_map/all_to_all | solution.py:90
  225.7 1.6 fusion.6
  227.3 13.1 %all-to-all-done.1 = bf16[64,8,128]{2,1,0:T(8,128)(2,1)S(1)} async-done(((bf16[64,8,128]{2,1,0:T(8,128)(2,1)}), bf16[64,8,128]{2,1,0:T(8,128)(2,1)S(1)}, u32[]{:S(2)}, u32[]{:S(2)}) %all-to-all-start.1) | async-done | bytes 131104 | tf_op jit(solution)/shard_map/all_to_all | solution.py:90
  252.8 6.7 copy.55
  260.0 46.6 %reduce = bf16[8192,8]{1,0:T(8,128)(2,1)} reduce(bf16[8192,1,8]{2,1,0:T(2,128)(2,1)} %bitcast.122, bf16[]{:T(256)} %broadcast.142), dimensions={1}, to_apply=%bitcast.104.reduce_sub_computation | reduce | bytes 262146
  306.6 4.3 reshape.131
  310.9 4.6 all-to-all-start.2
  316.3 13.9 %all-to-all-done.2 = bf16[64,2,512]{2,1,0:T(2,128)(2,1)S(1)} async-done(((bf16[64,2,512]{2,1,0:T(2,128)(2,1)}), bf16[64,2,512]{2,1,0:T(2,128)(2,1)S(1)}, u32[]{:S(2)}, u32[]{:S(2)}) %all-to-all-start.2) | async-done | bytes 131104 | tf_op jit(solution)/shard_map/all_to_all | solution.py:104
  330.2 8.7 %reshape.132 = bf16[8192,1,8]{2,1,0:T(2,128)(2,1)} reshape(bf16[64,2,512]{2,1,0:T(2,128)(2,1)S(1)} %all-to-all-done.2) | data formatting | bytes 262144
  338.9 8.5 %bitcast_convert_fusion = f32[1,8,8192]{1,0,2:T(1,128)} fusion(bf16[8192,1,8]{2,1,0:T(2,128)(2,1)} %reshape.132), kind=kLoop, calls=%fused_computation.195 | loop fusion | flops 65536 | bytes 393216 | tf_op jit(solution)/shard_map/convert_element_type | solution.py:109
  347.4 2.8 copy.56
  353.2 2.4 copy.76
  355.6 2.3 pad.9
  357.9 8.0 reshape.124
  365.9 3.3 reduce_sum.9
  369.4 436.5 %psum.7 = f32[32,128]{1,0:T(8,128)S(1)} all-reduce(f32[32,128]{1,0:T(8,128)S(1)} %rev.8), channel_id=1, replica_groups=mesh['seq'=64,'ch'=8] {'seq'}, use_global_device_ids=true, to_apply=%region_1.2 | all-reduce | flops 4096 | bytes 32768 | tf_op jit(solution)/shard_map/psum | solution.py:122
  (66 shorter events, 27.2 us)
Async XLA Ops:
  7.2 43.0 %all-gather.5.cloned.1.call-start = ((), (), s32[]{:S(2)}) async-start(), calls=%async_computation.4 | async-start | bytes 1179648 | tf_op jit(solution)/shard_map/all_gather | solution.py:77
  7.9 203.3 %all-gather.3.cloned.1.call-start = ((), (), s32[]{:S(2)}) async-start(), calls=%async_computation.3 | async-start | bytes 4259840 | tf_op jit(solution)/shard_map/all_gather | solution.py:79
  8.6 33.2 %collective-permute-start = (bf16[512,128]{1,0:T(8,128)(2,1)}, bf16[512,128]{1,0:T(8,128)(2,1)S(1)}, u32[]{:S(2)}, u32[]{:S(2)}) collective-permute-start(bf16[512,128]{1,0:T(8,128)(2,1)} %param.9), channel_id=1, source_target_pairs={{0,8},{8,16},{16,24},{24,32},{32,40},{40,48},{48,56},{56,64},{64,7... | collective-permute-start | bytes 393224 | tf_op jit(solution)/shard_map/ppermute | solution.py:13
  14.6 32.1 %all-to-all-start = ((bf16[64,8,128]{2,1,0:T(8,128)(2,1)}), bf16[64,8,128]{2,1,0:T(8,128)(2,1)S(1)}, u32[]{:S(2)}, u32[]{:S(2)}) async-start(bf16[64,8,128]{2,1,0:T(8,128)(2,1)} %bitcast.129), calls=%async_computation | async-start | bytes 262144 | tf_op jit(solution)/shard_map/all_to_all | solution.py:91
  39.7 1.6 slice-start
  39.7 2.1 copy-start.6
  42.4 1.0 copy-start.2
  215.7 24.7 %all-to-all-start.1 = ((bf16[64,8,128]{2,1,0:T(8,128)(2,1)}), bf16[64,8,128]{2,1,0:T(8,128)(2,1)S(1)}, u32[]{:S(2)}, u32[]{:S(2)}) async-start(bf16[64,8,128]{2,1,0:T(8,128)(2,1)} %fusion.5), calls=%async_computation.1 | async-start | bytes 262144 | tf_op jit(solution)/shard_map/all_to_all | solution.py:90
  240.9 5.4 copy-start
  240.9 5.4 copy-start.1
  260.0 55.6 %copy-start.4 = (bf16[32,16,1,256]{3,1,0,2:T(8,128)(2,1)S(1)}, bf16[32,16,1,256]{3,1,0,2:T(8,128)(2,1)}, u32[]{:S(2)}) copy-start(bf16[32,16,1,256]{3,1,0,2:T(8,128)(2,1)} %rev.7) | copy-start | bytes 786436
  310.9 19.3 %all-to-all-start.2 = ((bf16[64,2,512]{2,1,0:T(2,128)(2,1)}), bf16[64,2,512]{2,1,0:T(2,128)(2,1)S(1)}, u32[]{:S(2)}, u32[]{:S(2)}) async-start(bf16[64,2,512]{2,1,0:T(2,128)(2,1)} %reshape.131), calls=%async_computation.2 | async-start | bytes 262144 | tf_op jit(solution)/shard_map/all_to_all | solution.py:104
  347.4 2.8 copy-start.5
  347.4 5.1 copy-start.3
  350.9 455.6 %collective-permute-start.1 = (bf16[512,128]{1,0:T(8,128)(2,1)S(1)}, bf16[512,128]{1,0:T(8,128)(2,1)S(1)}, u32[]{:S(2)}, u32[]{:S(2)}) collective-permute-start(bf16[512,128]{1,0:T(8,128)(2,1)S(1)} %get-tuple-element.7), channel_id=1, source_target_pairs={{8,0},{16,8},{24,16},{32,24},{40,32},{48,40},{56,48},{64,56},{72,6... | collective-permute-start | bytes 393224 | tf_op jit(solution)/shard_map/ppermute | solution.py:13
Sparse Core Ops, SparseCore 0:
  10.0 38.5 all-gather.4
  53.0 158.1 all-gather.2
where the time goes:
time: 823 us; the launch traced here: 815 us
  blocking collectives  436 us (53%)
  waiting for transfers between devices  193 us (23%)
  other arithmetic  60 us (7%)
  local copies, waits for them, and re-layouts  49.3 us (6%)
  starting transfers between devices  37.8 us (5%)
  matrix products  24.5 us (3%)
  between operations  14.6 us (2%)
    psum x1, blocking collectives, local(): summed = lax.psum(local_part, 'seq')  436 us
    all_gather x1, waiting for transfers between devices, local(): lax.all_gather(out_weight, 'seq', axis=1, tiled=True)  161 us
    unnamed x1, other arithmetic  46.6 us
    dot_general x18, matrix products, contract(): return jnp.einsum(form, first, second, precision=highest)  17.3 us
    unnamed x22, local copies, waits for them, and re-layouts  16.5 us
  transfers between devices with their start and end apart: 7, of which 4 were waited for; matrix products, arithmetic and copies ran while one was open for 4% of the time, Pallas kernels for 0%

commit v1 on v0

--- a/solution.py
+++ b/solution.py
@@ -119,7 +119,8 @@
     skewed = flat.reshape(group_count, tap_count, 2 * tap_count + 1)
     column_sums = jnp.sum(skewed, axis=1)
     local_part = column_sums[:, 1 : tap_count + 1][:, ::-1]
-    summed = lax.psum(local_part, "seq")
+    pieces = lax.all_gather(local_part, "seq", axis=0, tiled=False)
+    summed = pieces.sum(axis=0)
     scale_factor = 1.0 / math.sqrt(row_count * seq_devices * per_group)
     return (d_key, d_value, summed * scale_factor)
 

time: 823 us -> 505 us (0.61)
  the two profiles are of different devices: /device:TPU:16 before, /device:TPU:2 now
where the time goes in v1:
time: 505 us; the launch traced here: 497 us
  waiting for transfers between devices  307 us (61%)
  other arithmetic  61.4 us (12%)
  local copies, waits for them, and re-layouts  50.1 us (10%)
  starting transfers between devices  39.9 us (8%)
  matrix products  24.5 us (5%)
  between operations  14.3 us (3%)
    all_gather x1, waiting for transfers between devices, local(): lax.all_gather(out_weight, 'seq', axis=1, tiled=True)  158 us
    all_gather x1, waiting for transfers between devices, local(): pieces = lax.all_gather(local_part, 'seq', axis=0, tiled=False)  109 us
    unnamed x1, other arithmetic  46.6 us
    dot_general x18, matrix products, contract(): return jnp.einsum(form, first, second, precision=highest)  17.3 us
    unnamed x22, local copies, waits for them, and re-layouts  16.7 us
    all_to_all x1, starting transfers between devices, local(): lax.all_to_all(packed[1], 'seq', split_axis=0, concat_axis=2, tiled=True)  14.1 us
    all_to_all x1, waiting for transfers between devices, local(): back = lax.all_to_all(d_w, 'seq', split_axis=2, concat_axis=0, tiled=True)  12.9 us
    ppermute x2, starting transfers between devices, from_behind(): lax.ppermute(value, axis, [(source, source + steps) for source in range(f...  11.8 us
  transfers between devices with their start and end apart: 8, of which 7 were waited for; matrix products, arithmetic and copies ran while one was open for 4% of the time, Pallas kernels for 0%

profile of v1, /device:TPU:2, one launch (start us, length us, event | category | flops | bytes accessed | tf_op | source)
XLA Modules:
  0.0 497.4 jit_solution(875422276125203666)
XLA Ops:
  8.6 7.7 %collective-permute-start = (bf16[512,128]{1,0:T(8,128)(2,1)}, bf16[512,128]{1,0:T(8,128)(2,1)S(1)}, u32[]{:S(2)}, u32[]{:S(2)}) collective-permute-start(bf16[512,128]{1,0:T(8,128)(2,1)} %param.9), channel_id=1, source_target_pairs={{0,8},{8,16},{16,24},{24,32},{32,40},{40,48},{48,56},{56,64},{64,7... | collective-permute-start | bytes 393224 | tf_op jit(solution)/shard_map/ppermute | solution.py:13
  16.4 14.1 %all-to-all-start = ((bf16[64,8,128]{2,1,0:T(8,128)(2,1)}), bf16[64,8,128]{2,1,0:T(8,128)(2,1)S(1)}, u32[]{:S(2)}, u32[]{:S(2)}) async-start(bf16[64,8,128]{2,1,0:T(8,128)(2,1)} %bitcast.131), calls=%async_computation | async-start | bytes 262144 | tf_op jit(solution)/shard_map/all_to_all | solution.py:91
  33.6 6.2 %tile.10 = bf16[32,32896]{1,0:T(8,128)(2,1)} reshape(bf16[32,128,257]{2,1,0:T(8,128)(2,1)} %tile.4) | data formatting | bytes 4210688 | tf_op jit(solution)/shard_map/tile | solution.py:98
  43.5 2.7 all-to-all-done
  49.7 5.2 %all-gather.7.cloned.1.call-done = bf16[4096,128]{1,0:T(8,128)(2,1)} async-done(((bf16[512,128]{1,0:T(8,128)(2,1)}), bf16[4096,128]{1,0:T(8,128)(2,1)}) %all-gather.7.cloned.1.call-update) | async-done | bytes 1048592 | tf_op jit(solution)/shard_map/all_gather | solution.py:77
  54.9 158.1 %all-gather.5.cloned.1.call-done = bf16[512,4096]{0,1:T(8,128)(2,1)} async-done(((bf16[512,64]{0,1:T(8,128)(2,1)}), bf16[512,4096]{0,1:T(8,128)(2,1)}) %all-gather.5.cloned.1.call-update) | async-done | bytes 4194320 | tf_op jit(solution)/shard_map/all_gather | solution.py:79
  213.0 4.5 fusion.5
  217.5 8.4 %all-to-all-start.1 = ((bf16[64,8,128]{2,1,0:T(8,128)(2,1)}), bf16[64,8,128]{2,1,0:T(8,128)(2,1)S(1)}, u32[]{:S(2)}, u32[]{:S(2)}) async-start(bf16[64,8,128]{2,1,0:T(8,128)(2,1)} %fusion.5), calls=%async_computation.1 | async-start | bytes 262144 | tf_op jit(solution)/shard_map/all_to_all | solution.py:90
  227.5 11.6 %all-to-all-done.1 = bf16[64,8,128]{2,1,0:T(8,128)(2,1)S(1)} async-done(((bf16[64,8,128]{2,1,0:T(8,128)(2,1)}), bf16[64,8,128]{2,1,0:T(8,128)(2,1)S(1)}, u32[]{:S(2)}, u32[]{:S(2)}) %all-to-all-start.1) | async-done | bytes 131104 | tf_op jit(solution)/shard_map/all_to_all | solution.py:90
  251.4 6.8 %copy.75 = bf16[1,8,8192]{1,0,2:T(2,128)(2,1)} copy(bf16[1,8,8192]{2,1,0:T(8,128)(2,1)S(1)} %convert_element_type.134) | data formatting | bytes 262144 | tf_op jit(solution)/shard_map/convert_element_type | solution.py:62
  258.6 46.6 %reduce = bf16[8192,8]{1,0:T(8,128)(2,1)} reduce(bf16[8192,1,8]{2,1,0:T(2,128)(2,1)} %bitcast.123, bf16[]{:T(256)} %broadcast.142), dimensions={1}, to_apply=%bitcast.105.reduce_sub_computation | reduce | bytes 262146
  305.2 4.3 reshape.132
  309.6 5.5 %all-to-all-start.2 = ((bf16[64,2,512]{2,1,0:T(2,128)(2,1)}), bf16[64,2,512]{2,1,0:T(2,128)(2,1)S(1)}, u32[]{:S(2)}, u32[]{:S(2)}) async-start(bf16[64,2,512]{2,1,0:T(2,128)(2,1)} %reshape.132), calls=%async_computation.2 | async-start | bytes 262144 | tf_op jit(solution)/shard_map/all_to_all | solution.py:104
  315.9 12.9 %all-to-all-done.2 = bf16[64,2,512]{2,1,0:T(2,128)(2,1)S(1)} async-done(((bf16[64,2,512]{2,1,0:T(2,128)(2,1)}), bf16[64,2,512]{2,1,0:T(2,128)(2,1)S(1)}, u32[]{:S(2)}, u32[]{:S(2)}) %all-to-all-start.2) | async-done | bytes 131104 | tf_op jit(solution)/shard_map/all_to_all | solution.py:104
  328.8 8.9 %reshape.133 = bf16[8192,1,8]{2,1,0:T(2,128)(2,1)} reshape(bf16[64,2,512]{2,1,0:T(2,128)(2,1)S(1)} %all-to-all-done.2) | data formatting | bytes 262144
  337.7 8.5 %bitcast_convert_fusion = f32[1,8,8192]{1,0,2:T(1,128)} fusion(bf16[8192,1,8]{2,1,0:T(2,128)(2,1)} %reshape.133), kind=kLoop, calls=%fused_computation.195 | loop fusion | flops 65536 | bytes 393216 | tf_op jit(solution)/shard_map/convert_element_type | solution.py:109
  346.2 2.8 copy.76
  350.5 2.4 copy.96
  353.0 2.3 pad.9
  355.3 8.0 %reshape.124 = f32[32,128,257]{2,1,0:T(8,128)} reshape(f32[32,32896]{1,0:T(8,128)} %pad.9) | data formatting | bytes 8421376 | tf_op jit(solution)/shard_map/reshape | solution.py:119
  363.3 3.3 reduce_sum.18
  367.4 4.1 collective-permute-start.1
  371.5 6.8 %collective-permute-done.1 = bf16[512,128]{1,0:T(8,128)(2,1)S(1)} collective-permute-done((bf16[512,128]{1,0:T(8,128)(2,1)S(1)}, bf16[512,128]{1,0:T(8,128)(2,1)S(1)}, u32[]{:S(2)}, u32[]{:S(2)}) %collective-permute-start.1) | collective-permute-done | bytes 131104 | tf_op jit(solution)/shard_map/ppermute | solution.py:13
  380.1 108.6 %all-gather.9.cloned.1.call-done = f32[2048,128]{1,0:T(8,128)} async-done(((f32[32,128]{1,0:T(8,128)}), f32[2048,128]{1,0:T(8,128)}) %all-gather.9.cloned.1.call-update) | async-done | bytes 1048592 | tf_op jit(solution)/shard_map/all_gather | solution.py:122
  (69 shorter events, 32.9 us)
Async XLA Ops:
  7.2 47.7 %all-gather.7.cloned.1.call-start = ((), (), s32[]{:S(2)}) async-start(), calls=%async_computation.4 | async-start | bytes 1179648 | tf_op jit(solution)/shard_map/all_gather | solution.py:77
  7.9 205.1 %all-gather.5.cloned.1.call-start = ((), (), s32[]{:S(2)}) async-start(), calls=%async_computation.3 | async-start | bytes 4259840 | tf_op jit(solution)/shard_map/all_gather | solution.py:79
  8.6 33.3 %collective-permute-start = (bf16[512,128]{1,0:T(8,128)(2,1)}, bf16[512,128]{1,0:T(8,128)(2,1)S(1)}, u32[]{:S(2)}, u32[]{:S(2)}) collective-permute-start(bf16[512,128]{1,0:T(8,128)(2,1)} %param.9), channel_id=1, source_target_pairs={{0,8},{8,16},{16,24},{24,32},{32,40},{40,48},{48,56},{56,64},{64,7... | collective-permute-start | bytes 393224 | tf_op jit(solution)/shard_map/ppermute | solution.py:13
  16.4 29.8 %all-to-all-start = ((bf16[64,8,128]{2,1,0:T(8,128)(2,1)}), bf16[64,8,128]{2,1,0:T(8,128)(2,1)S(1)}, u32[]{:S(2)}, u32[]{:S(2)}) async-start(bf16[64,8,128]{2,1,0:T(8,128)(2,1)} %bitcast.131), calls=%async_computation | async-start | bytes 262144 | tf_op jit(solution)/shard_map/all_to_all | solution.py:91
  39.8 1.6 slice-start
  39.8 2.1 copy-start.6
  42.5 1.0 copy-start.2
  217.5 21.6 %all-to-all-start.1 = ((bf16[64,8,128]{2,1,0:T(8,128)(2,1)}), bf16[64,8,128]{2,1,0:T(8,128)(2,1)S(1)}, u32[]{:S(2)}, u32[]{:S(2)}) async-start(bf16[64,8,128]{2,1,0:T(8,128)(2,1)} %fusion.5), calls=%async_computation.1 | async-start | bytes 262144 | tf_op jit(solution)/shard_map/all_to_all | solution.py:90
  239.6 5.4 %copy-start = (f32[8,128,128]{2,1,0:T(8,128)S(1)}, f32[8,128,128]{2,1,0:T(8,128)}, u32[]{:S(2)}) copy-start(f32[8,128,128]{2,1,0:T(8,128)} %convolution_add_fusion.2) | copy-start | bytes 1572868
  239.6 5.4 %copy-start.1 = (f32[8,128,128]{2,1,0:T(8,128)S(1)}, f32[8,128,128]{2,1,0:T(8,128)}, u32[]{:S(2)}) copy-start(f32[8,128,128]{2,1,0:T(8,128)} %fusion.6) | copy-start | bytes 1572868
  258.6 56.5 %copy-start.4 = (bf16[32,16,1,256]{3,1,0,2:T(8,128)(2,1)S(1)}, bf16[32,16,1,256]{3,1,0,2:T(8,128)(2,1)}, u32[]{:S(2)}) copy-start(bf16[32,16,1,256]{3,1,0,2:T(8,128)(2,1)} %rev.7) | copy-start | bytes 786436
  309.6 19.3 %all-to-all-start.2 = ((bf16[64,2,512]{2,1,0:T(2,128)(2,1)}), bf16[64,2,512]{2,1,0:T(2,128)(2,1)S(1)}, u32[]{:S(2)}, u32[]{:S(2)}) async-start(bf16[64,2,512]{2,1,0:T(2,128)(2,1)} %reshape.132), calls=%async_computation.2 | async-start | bytes 262144 | tf_op jit(solution)/shard_map/all_to_all | solution.py:104
  315.1 173.7 %all-gather.9.cloned.1.call-start = ((), (), s32[]{:S(2)}) async-start(), calls=%async_computation.5 | async-start | bytes 1064960 | tf_op jit(solution)/shard_map/all_gather | solution.py:122
  346.2 2.8 copy-start.5
  346.2 3.6 copy-start.3
  367.4 10.8 %collective-permute-start.1 = (bf16[512,128]{1,0:T(8,128)(2,1)S(1)}, bf16[512,128]{1,0:T(8,128)(2,1)S(1)}, u32[]{:S(2)}, u32[]{:S(2)}) collective-permute-start(bf16[512,128]{1,0:T(8,128)(2,1)S(1)} %get-tuple-element.7), channel_id=1, source_target_pairs={{8,0},{16,8},{24,16},{32,24},{40,32},{48,40},{56,48},{64,56},{72,6... | collective-permute-start | bytes 393224 | tf_op jit(solution)/shard_map/ppermute | solution.py:13
Sparse Core Ops, SparseCore 0:
  10.0 44.7 all-gather.6
  59.2 153.7 all-gather.4
  367.5 121.1 all-gather.8
